TPU v7x, 32 devices: a whole 2x2x4 slice. The times are simulated.
32 devices in a mesh: group: 2 (over x), replica: 16 (over z, y, core).
Axes of the slice: x: 2, y: 2, z: 4, core: 2. Of those that a mesh axis runs over, the one named last changes fastest.
Arguments:
- tokens: bfloat16 [32, 1024, 768], P(('group', 'replica')), may hold values from -6 to 6
- lengths: int32 [32], P(('group', 'replica')), may hold values from 256 to 1024, as said below
- w_qkv: bfloat16 [768, 2304], P('group'), may hold values from -0.21875 to 0.21875
- w_out: bfloat16 [768, 768], P('group'), may hold values from -4 to 4
- gain_one: bfloat16 [768], P('group'), may hold values from 0.25 to 1.75
- w_in: bfloat16 [768, 2304], P('group'), may hold values from -0.21875 to 0.21875
- w_down: bfloat16 [1152, 768], P('group'), may hold values from -0.1875 to 0.1875
- gain_two: bfloat16 [768], P('group'), may hold values from 0.25 to 1.75
- cotangent: bfloat16 [32, 1024, 768], P(('group', 'replica')), may hold values from -6 to 6
Outputs:
- output: bfloat16 [32, 1024, 768], P(('group', 'replica'))
- grad_tokens: float32 [32, 1024, 768], P(('group', 'replica'))
- grad_qkv: float32 [768, 2304], P('group')
- grad_out: float32 [768, 768], P('group')
- grad_gain_one: float32 [768], P('group')
- grad_in: float32 [768, 2304], P('group')
- grad_down: float32 [1152, 768], P('group')
- grad_gain_two: float32 [768], P('group')
Inputs may be any that keep to these rules, and one draw needn't show every extreme that they name: Slots 0 to lengths - 1 of a sequence hold tokens, the rest are padding; some sequence has exactly 1024 valid slots and some exactly 256.
All inputs are finite; a program needn't handle non-finite values.
Results may differ from a plain program's by a relative error of at most 0.018.
Values may be sent and summed in bfloat16 or wider, within the bound.
No kernel may reach another device: no remote copies, remote signals or barrier semaphores. Data moves between devices by JAX's collectives and lax.ppermute only.
A program may use at most 192 MiB of HBM per device.

v0:
```python
import math
import jax
import jax.numpy as jnp
from jax import lax
from jax.sharding import PartitionSpec as P

HEADS = 12
HEAD_DIM = 64
theta_base = 160000.0
norm_eps = 1e-05


def normed(field, gain):
    center = field - jnp.mean(field, axis=-1, keepdims=True)
    spread = jnp.mean(center * center, axis=-1, keepdims=True)
    return center * lax.rsqrt(spread + norm_eps) * gain


def rotary(field):
    half = HEAD_DIM // 2
    length = field.shape[1]
    freq = jnp.exp(-math.log(theta_base) * 2.0 * jnp.arange(half, dtype=jnp.float32) / HEAD_DIM)
    angle = jnp.arange(length, dtype=jnp.float32)[:, None] * freq[None, :]
    cosine = jnp.cos(angle)
    sine = jnp.sin(angle)
    first = field[..., :half]
    second = field[..., half:]
    return jnp.concatenate(
        [first * cosine - second * sine, second * cosine + first * sine], axis=-1
    )


def rotate_both(query, key_rows):
    return (rotary(query), rotary(key_rows))


def geglu(upward):
    half = upward.shape[1] // 2
    return jax.nn.gelu(upward[:, :half], approximate=False) * upward[:, half:]


def inner(left, right):
    return lax.dot_general(
        left, right, (((0,), (0,)), ((), ())), preferred_element_type=jnp.float32
    )


def outer(left, right):
    return lax.dot_general(
        left, right, (((1,), (1,)), ((), ())), preferred_element_type=jnp.float32
    )


def swap_replica(field, bit):
    count = lax.axis_size("replica")
    return lax.ppermute(field, "replica", [(i, i ^ bit) for i in range(count)])


def swap_group(field):
    return lax.ppermute(field, "group", [(0, 1), (1, 0)])


def pick(field, index, axis):
    size = field.shape[axis] // 2
    return lax.dynamic_slice_in_dim(field, index * size, size, axis)


def in_order(mine, other, index, axis):
    return jnp.where(
        index == 0,
        jnp.concatenate([mine, other], axis=axis),
        jnp.concatenate([other, mine], axis=axis),
    )


def add_low(left, right):
    return (left.astype(jnp.float32) + right.astype(jnp.float32)).astype(jnp.bfloat16)


def other_rows(send, core):
    fetched = swap_group(send)
    return (fetched, swap_replica(fetched, 1))


def reduce_unit(send, keep, group, replica):
    count = lax.axis_size("replica")
    total = add_low(keep, swap_replica(send, 1))
    total = add_low(pick(total, group, 0), swap_group(pick(total, 1 - group, 0)))[0]
    split = []
    bit = 2
    while bit < count:
        at = replica // bit % 2
        if total.shape[0] % 32 == 0:
            total = add_low(pick(total, at, 0), swap_replica(pick(total, 1 - at, 0), bit))
            split.append((bit, at))
        else:
            total = add_low(total, swap_replica(total, bit))
        bit *= 2
    for bit, at in reversed(split):
        total = in_order(total, swap_replica(total, bit), at, 0)
    return (total, swap_replica(total, 1))


def on_device(tokens, lengths, w_qkv, w_out, gain_one, w_in, w_down, gain_two, cotangent):
    field = tokens[0].astype(jnp.float32)
    length = field.shape[0]
    width = field.shape[1]
    scale = 1.0 / math.sqrt(HEAD_DIM)
    valid = jnp.arange(length, dtype=jnp.int32) < lengths[0]
    group = lax.axis_index("group")
    replica = lax.axis_index("replica")
    core = replica % 2
    gain_rows = jnp.zeros((16, w_qkv.shape[1] // 2), jnp.bfloat16)
    gain_rows = lax.dynamic_update_slice(gain_rows, gain_one[None], (0, 0))
    qkv_send = jnp.concatenate([pick(w_qkv, core, 1), gain_rows], axis=0)
    rest_rows = jnp.zeros((16, w_out.shape[1] // 2), jnp.bfloat16)
    rest_rows = lax.dynamic_update_slice(rest_rows, gain_two[None], (0, 0))
    wide = w_out.shape[1] // 2
    in_half = pick(w_in, core, 1)
    rest_send = jnp.concatenate(
        [pick(w_out, core, 1), pick(w_down, core, 1)]
        + [in_half[:, i * wide : (i + 1) * wide] for i in range(3)]
        + [rest_rows],
        axis=0,
    )
    qkv_parts = other_rows(qkv_send, core)
    rest_parts = other_rows(rest_send, core)
    n_own = w_qkv.shape[0]
    n_down = w_down.shape[0]
    cut = [0, n_own, n_own + n_down, 2 * n_own + n_down, 3 * n_own + n_down, 4 * n_own + n_down]

    def whole(own, parts):
        return in_order(own, in_order(parts[0], parts[1], core, 1), group, 0)

    qkv_full = whole(w_qkv, [part[:n_own] for part in qkv_parts])
    gain_first = in_order(gain_one, qkv_parts[0][n_own, :n_own], group, 0)
    out_full = whole(w_out, [part[: cut[1]] for part in rest_parts])
    down_full = whole(w_down, [part[cut[1] : cut[2]] for part in rest_parts])
    in_full = whole(
        w_in,
        [
            jnp.concatenate([part[cut[i] : cut[i + 1]] for i in (2, 3, 4)], axis=1)
            for part in rest_parts
        ],
    )
    gain_second = in_order(gain_two, rest_parts[0][cut[5], :n_own], group, 0)
    first_f, first_pull = jax.vjp(normed, field, gain_first.astype(jnp.float32))
    first_in = first_f.astype(jnp.bfloat16)
    merged = jnp.dot(first_in, qkv_full, preferred_element_type=jnp.float32)
    parts = merged.reshape(length, 3, HEADS, HEAD_DIM).transpose(1, 2, 0, 3)
    (query_f, key_f), rotate_pull = jax.vjp(rotate_both, parts[0], parts[1])
    query = query_f.astype(jnp.bfloat16)
    key_rows = key_f.astype(jnp.bfloat16)
    values = parts[2].astype(jnp.bfloat16)

    def masked_scores(head_query, head_keys):
        scores = (
            jnp.einsum("qd,kd->qk", head_query, head_keys, preferred_element_type=jnp.float32)
            * scale
        )
        return jnp.where(valid[None, :], scores, -1e30)

    def forward_head(item):
        head_query, head_keys, head_values = item
        scores = masked_scores(head_query, head_keys)
        top = jnp.max(scores, axis=1, keepdims=True)
        weights = jnp.exp(scores - top)
        total = jnp.sum(weights, axis=1, keepdims=True)
        weights = weights / total
        result = jnp.einsum(
            "qk,kd->qd",
            weights.astype(jnp.bfloat16),
            head_values,
            preferred_element_type=jnp.float32,
        )
        return (result, top[:, 0] + jnp.log(total[:, 0]))

    heads, log_totals = lax.map(forward_head, (query, key_rows, values))
    mixed = heads.transpose(1, 0, 2).reshape(length, width).astype(jnp.bfloat16)
    middle = field + jnp.dot(mixed, out_full, preferred_element_type=jnp.float32)
    second_f, second_pull = jax.vjp(normed, middle, gain_second.astype(jnp.float32))
    second_in = second_f.astype(jnp.bfloat16)
    upward = jnp.dot(second_in, in_full, preferred_element_type=jnp.float32)
    activ_f, activ_pull = jax.vjp(geglu, upward)
    activ = activ_f.astype(jnp.bfloat16)
    result = middle + jnp.dot(activ, down_full, preferred_element_type=jnp.float32)
    output = jnp.where(valid[:, None], result, 0.0).astype(jnp.bfloat16)[None]
    d_out = jnp.where(valid[:, None], cotangent[0], jnp.zeros((), jnp.bfloat16))
    grad_down = inner(activ, d_out)
    d_activ = outer(d_out, down_full)
    (d_up,) = activ_pull(d_activ)
    d_up = d_up.astype(jnp.bfloat16)
    grad_in = inner(second_in, d_up)
    d_second = outer(d_up, in_full)
    d_middle_norm, grad_gain_two = second_pull(d_second)
    d_middle = d_out.astype(jnp.float32) + d_middle_norm
    d_middle_low = d_middle.astype(jnp.bfloat16)
    grad_out = inner(mixed, d_middle_low)
    d_mixed = outer(d_middle_low, out_full).astype(jnp.bfloat16)
    d_heads = d_mixed.reshape(length, HEADS, HEAD_DIM).transpose(1, 0, 2)

    def backward_head(item):
        head_query, head_keys, head_values, head_grad, log_total = item
        scores = masked_scores(head_query, head_keys)
        weights = jnp.where(valid[None, :], jnp.exp(scores - log_total[:, None]), 0.0)
        d_values = jnp.einsum(
            "qk,qd->kd", weights.astype(jnp.bfloat16), head_grad, preferred_element_type=jnp.float32
        )
        d_weights = jnp.einsum(
            "qd,kd->qk", head_grad, head_values, preferred_element_type=jnp.float32
        )
        d_scores = weights * (d_weights - jnp.sum(weights * d_weights, axis=1, keepdims=True))
        d_scores = d_scores.astype(jnp.bfloat16)
        d_query = (
            jnp.einsum("qk,kd->qd", d_scores, head_keys, preferred_element_type=jnp.float32) * scale
        )
        d_keys = (
            jnp.einsum("qk,qd->kd", d_scores, head_query, preferred_element_type=jnp.float32)
            * scale
        )
        return (d_query, d_keys, d_values)

    d_query_r, d_keys_r, d_values = lax.map(
        backward_head, (query, key_rows, values, d_heads, log_totals)
    )
    d_query, d_keys = rotate_pull((d_query_r, d_keys_r))
    d_merged = (
        jnp.stack([d_query, d_keys, d_values]).transpose(2, 0, 1, 3).reshape(length, 3 * width)
    )
    d_merged = d_merged.astype(jnp.bfloat16)
    grad_qkv = inner(first_in, d_merged)
    d_first = outer(d_merged, qkv_full)
    d_field_norm, grad_gain_one = first_pull(d_first)
    grad_tokens = (d_middle + d_field_norm)[None]

    def unit_of(fields):
        halves = []
        for half in (1 - core, core):
            parts = []
            for field in fields:
                part = pick(field.astype(jnp.bfloat16), half, 1)
                rows = part.shape[0] // 2
                for i in range(part.shape[1] // wide):
                    parts.append(part[:, i * wide : (i + 1) * wide].reshape(2, rows, wide))
            used = sum((part.shape[1] for part in parts))
            filled = -(-used // 128) * 128
            if filled > used:
                parts.append(jnp.zeros((2, filled - used, wide), jnp.bfloat16))
            halves.append(jnp.concatenate(parts, axis=1))
        return halves

    def gain_unit(field):
        return (
            jnp.zeros((2 * n_own, 2 * wide), jnp.float32)
            .at[:2, :n_own]
            .set(field.reshape(2, n_own))
        )

    def spread(result, fields):
        outs = []
        at = 0
        for field in fields:
            rows = field.shape[0] // 2
            count = field.shape[1] // 2 // wide
            sides = []
            for side in result:
                sides.append(
                    jnp.concatenate(
                        [side[at + i * rows : at + (i + 1) * rows] for i in range(count)], axis=1
                    )
                )
            outs.append(in_order(sides[0], sides[1], core, 1).astype(jnp.float32))
            at += rows * count
        return outs

    early = [grad_down, grad_in, grad_out]
    early_sum = reduce_unit(*unit_of(early), group, replica)
    late = [grad_qkv]
    late_sum = reduce_unit(*unit_of(late), group, replica)
    grad_down, grad_in, grad_out = spread(early_sum, early)
    (grad_qkv,) = spread(late_sum, late)
    gains = jnp.stack([grad_gain_one, grad_gain_two])
    gains = lax.psum(gains, ("group", "replica"))
    gains = lax.dynamic_slice_in_dim(gains, group * n_own, n_own, 1)
    return (output, grad_tokens, grad_qkv, grad_out, gains[0], grad_in, grad_down, gains[1])


def solution(mesh):
    in_specs = (
        P(("group", "replica"), None, None),
        P(("group", "replica")),
        P("group", None),
        P("group", None),
        P("group"),
        P("group", None),
        P("group", None),
        P("group"),
        P(("group", "replica"), None, None),
    )
    out_specs = (
        P(("group", "replica"), None, None),
        P(("group", "replica"), None, None),
        P("group", None),
        P("group", None),
        P("group"),
        P("group", None),
        P("group", None),
        P("group"),
    )
    return jax.shard_map(
        on_device, mesh=mesh, in_specs=in_specs, out_specs=out_specs, check_vma=False
    )
```

profile of v0, /device:TPU:1, one launch (start us, length us, event | category | flops | bytes accessed | tf_op | source)
XLA Modules:
  0.0 799.1 jit_solution(9865017861474288771)
XLA Ops:
  11.8 4.3 copy.179
  18.3 3.9 copy.195
  34.1 27.3 %collective-permute-done.2 = bf16[2128,384]{1,0:T(8,128)(2,1)} collective-permute-done((bf16[2128,384]{1,0:T(8,128)(2,1)}, bf16[2128,384]{1,0:T(8,128)(2,1)}, u32[]{:S(2)}, u32[]{:S(2)}) %collective-permute-start.2) | collective-permute-done | bytes 1634336 | tf_op jit(solution)/shard_map/ppermute | solution.py:60
  80.1 4.1 convolution_bitcast_fusion
  96.5 4.3 copy.184
  100.8 123.5 %while.30 = (s32[]{:T(128)}, bf16[12,1024,64]{1,2,0:T(8,128)(2,1)S(1)}, f32[12,1024]{1,0:T(8,128)}, bf16[12,1024,64]{2,1,0:T(8,128)(2,1)}, bf16[12,1024,64]{2,1,...) while((s32[]{:T(128)}, bf16[12,1024,64]{1,2,0:T(8,128)(2,1)S(1)}, ...), condition=%wide.region_5.6_spmd.clone.clone, body=%wide.region_2.5_spmd.clone.sunk.clone | while | flops 281018368 | bytes 30455920 | solution.py:178
  117.9 3.5 fusion.162
  138.5 3.5 fusion.162
  247.4 4.3 fusion.87
  251.7 14.9 %fusion.78 = (f32[1024,1152]{1,0:T(8,128)}, f32[1024,1152]{1,0:T(8,128)S(1)}, f32[1024,1152]{1,0:T(8,128)S(1)}) fusion(f32[1024,2304]{1,0:T(8,128)S(1)} %fusion.87, bf16[576,768]{0,1:T(8,128)(2,1)S(1)} %maximum_select_fusion.6, bf16[576,768]{0,1:T(8,128)(2,1)S(1)} %copy-done.44, pred[]{:T(512)S(6)} %eq.18, bf16[1,1024,768]{1,2,0:T(8,128)(2,1)S(1)} %copy-done.8, ...), kind=kOutput, calls=%fused_computation.147 | convolution fusion | flops 1897365504 | bytes 22217728 | tf_op jit(solution)/shard_map/dot_general | solution.py:49
  266.7 4.5 multiply_add_fusion
  271.2 11.5 %multiply_reduce_fusion.1 = (f32[768]{0:T(1024)}, f32[1024]{0:T(1024)S(1)}, f32[1024,768]{0,1:T(8,128)}) fusion(f32[1024,768]{0,1:T(8,128)S(1)} %copy-done.13, f32[1024]{0:T(1024)S(1)} %fusion.95, f32[1024]{0:T(1024)S(1)} %broadcast_multiply_fusion, f32[768]{0:T(1024)S(1)} %fusion.97, bf16[384,2304]{0,1:T(8,128)(2,1)} %copy-done.32, ...), kind=kOutput, calls=%fused_computation.109 | convolution fusion | flops 3650025728 | bytes 19286016 | tf_op jit(solution)/shard_map/dot_general | solution.py:49
  282.7 9.6 %convolution_convert_fusion = bf16[768,2304]{1,0:T(8,128)(2,1)} fusion(f32[1024,1152]{1,0:T(8,128)} %get-tuple-element.318, f32[1024,1152]{1,0:T(8,128)} %get-tuple-element.312, f32[1024,768]{0,1:T(8,128)S(1)} %copy-done.13, f32[768]{0:T(1024)S(1)} %fusion.97, f32[1024]{0:T(1024)S(1)} %fusion.95, f32[1024]{0:T(1024)S(1)} %broadcast_multiply_fusion), kind=kOutput, calls=%fused_computation.62 | convolution fusion | flops 3633512448 | bytes 16133120 | tf_op jit(solution)/shard_map/dot_general | solution.py:43
  298.0 4.2 copy.203
  302.2 160.5 %while.31 = (s32[]{:T(128)}, f32[12,1024,64]{1,2,0:T(8,128)}, f32[12,1024,64]{1,2,0:T(8,128)}, bf16[12,1024,64]{1,2,0:T(8,128)(2,1)S(1)}, bf16[12,1024,64]{2,1,0...) while((s32[]{:T(128)}, f32[12,1024,64]{1,2,0:T(8,128)}, ...), condition=%wide.region_12.13_spmd.clone.clone, body=%wide.region_10.12_spmd.clone.sunk.clone | while | flops 681705472 | bytes 34106476 | solution.py:223
  462.8 3.8 multiply_add_fusion.4
  467.8 4.8 convolution_convert_fusion.1
  496.1 3.7 convolution_convert_fusion.2
  503.5 6.9 concatenate.218
  523.2 19.9 %collective-permute-done.5 = bf16[1,1152,384]{1,2,0:T(8,128)(2,1)} collective-permute-done((bf16[1,1152,384]{1,2,0:T(8,128)(2,1)}, bf16[1,1152,384]{1,2,0:T(8,128)(2,1)}, u32[]{:S(2)}, u32[]{:S(2)}) %collective-permute-start.5) | collective-permute-done | bytes 884768 | tf_op jit(solution)/shard_map/ppermute | solution.py:60
  559.0 7.1 concatenate.217
  569.9 3.7 add_convert_fusion.1
  581.5 9.8 %fusion.66 = (f32[1024]{0:T(1024)}, f32[1024,768]{0,1:T(8,128)}) fusion(bf16[1,1024,768]{1,2,0:T(8,128)(2,1)S(1)} %copy.176, f32[768]{0:T(1024)S(1)} %copy-done.54, f32[1024]{0:T(1024)S(1)} %copy-done.50, bf16[1024,2304]{0,1:T(8,128)(2,1)} %bitcast.224, bf16[768,2304]{0,1:T(8,128)(2,1)} %copy-done.21), kind=kOutput, calls=%fused_computation.100 | convolution fusion | flops 3627809792 | bytes 12987392 | tf_op jit(solution)/shard_map/dot_general | solution.py:49
  591.7 21.8 %collective-permute-done.14 = bf16[1,2176,384]{1,2,0:T(8,128)(2,1)} collective-permute-done((bf16[1,2176,384]{1,2,0:T(8,128)(2,1)}, bf16[1,2176,384]{1,2,0:T(8,128)(2,1)}, u32[]{:S(2)}, u32[]{:S(2)}) %collective-permute-start.14) | collective-permute-done | bytes 1671200 | tf_op jit(solution)/shard_map/ppermute | solution.py:60
  620.2 7.1 fusion.79
  627.8 5.9 collective-permute-done.10
  644.4 6.6 collective-permute-done.16
  656.5 10.4 %collective-permute-start.12 = (bf16[1152,384]{0,1:T(8,128)(2,1)}, bf16[1152,384]{0,1:T(8,128)(2,1)}, u32[]{:S(2)}, u32[]{:S(2)}) collective-permute-start(bf16[1152,384]{0,1:T(8,128)(2,1)} %maximum_select_fusion.8), channel_id=1, source_target_pairs={{0,1},{1,0},{2,3},{3,2},{4,5},{5,4},{6,7},{7,6},{8,9},{9,8},{10,11... | collective-permute-start | bytes 2654216 | tf_op jit(solution)/shard_map/ppermute | solution.py:56
  667.2 9.3 %collective-permute-done.18 = bf16[272,384]{0,1:T(8,128)(2,1)S(1)} collective-permute-done((bf16[272,384]{0,1:T(8,128)(2,1)S(1)}, bf16[272,384]{0,1:T(8,128)(2,1)S(1)}, u32[]{:S(2)}, u32[]{:S(2)}) %collective-permute-start.18) | collective-permute-done | bytes 208928 | tf_op jit(solution)/shard_map/ppermute | solution.py:56
  681.1 3.7 copy.229
  686.3 47.6 %psum.7 = f32[2,768]{1,0:T(2,128)S(1)} all-reduce(f32[2,768]{1,0:T(2,128)S(1)} %pad_maximum_fusion.3), channel_id=1, replica_groups=mesh['group'=2,'replica'=16] {'group','replica'}, use_global_device_ids=true, to_apply=%region_17.18 | all-reduce | flops 1536 | bytes 12288 | tf_op jit(solution)/shard_map/psum | solution.py:283
  748.8 10.8 %collective-permute-done.20 = bf16[1088,384]{1,0:T(8,128)(2,1)} collective-permute-done((bf16[1088,384]{1,0:T(8,128)(2,1)S(1)}, bf16[1088,384]{1,0:T(8,128)(2,1)}, u32[]{:S(2)}, u32[]{:S(2)}) %collective-permute-start.20) | collective-permute-done | bytes 835616 | tf_op jit(solution)/shard_map/ppermute | solution.py:56
  (518 shorter events, 512.2 us)
Async XLA Ops:
  3.9 25.9 %collective-permute-start = (bf16[400,1152]{1,0:T(8,128)(2,1)}, bf16[400,1152]{1,0:T(8,128)(2,1)}, u32[]{:S(2)}, u32[]{:S(2)}) collective-permute-start(bf16[400,1152]{1,0:T(8,128)(2,1)} %fusion.83), channel_id=1, source_target_pairs={{0,16},{16,0},{1,17},{17,1},{2,18},{18,2},{3,19},{19,3},{4,20},{20... | collective-permute-start | bytes 2764808 | tf_op jit(solution)/shard_map/ppermute | solution.py:60
  10.3 51.1 %collective-permute-start.2 = (bf16[2128,384]{1,0:T(8,128)(2,1)}, bf16[2128,384]{1,0:T(8,128)(2,1)}, u32[]{:S(2)}, u32[]{:S(2)}) collective-permute-start(bf16[2128,384]{1,0:T(8,128)(2,1)} %constant_dynamic-update-slice_fusion), channel_id=1, source_target_pairs={{0,16},{16,0},{1,17},{17,1},{2,18},{18,2},{3,19},{19,3},{4,20},{20... | collective-permute-start | bytes 4902920 | tf_op jit(solution)/shard_map/ppermute | solution.py:60
  11.7 13.5 %copy-start.3 = (bf16[12,1024,64]{1,2,0:T(8,128)(2,1)}, bf16[12,1024,64]{1,2,0:T(8,128)(2,1)S(1)}, u32[]{:S(2)}) copy-start(bf16[12,1024,64]{1,2,0:T(8,128)(2,1)S(1)} %fusion.111) | copy-start | bytes 4718596
  28.1 50.2 %copy-start.49 = (f32[1024]{0:T(1024)}, f32[1024]{0:T(1024)S(1)}, u32[]{:S(2)}) copy-start(f32[1024]{0:T(1024)S(1)} %broadcast_multiply_fusion.1) | copy-start | bytes 12292
  29.8 56.9 %copy-start.36 = (f32[1024,32]{0,1:T(8,128)}, f32[1024,32]{0,1:T(8,128)S(1)}, u32[]{:S(2)}) copy-start(f32[1024,32]{0,1:T(8,128)S(1)} %get-tuple-element.381) | copy-start | bytes 393220
  29.8 40.7 %collective-permute-start.1 = (bf16[400,1152]{1,0:T(8,128)(2,1)}, bf16[400,1152]{1,0:T(8,128)(2,1)}, u32[]{:S(2)}, u32[]{:S(2)}) collective-permute-start(bf16[400,1152]{1,0:T(8,128)(2,1)} %collective-permute-done), channel_id=1, source_target_pairs={{0,1},{1,0},{2,3},{3,2},{4,5},{5,4},{6,7},{7,6},{8,9},{9,8},{10,11... | collective-permute-start | bytes 2764808 | tf_op jit(solution)/shard_map/ppermute | solution.py:56
  30.8 47.6 %copy-start.51 = (f32[1024]{0:T(1024)}, f32[1024]{0:T(1024)S(1)}, u32[]{:S(2)}) copy-start(f32[1024]{0:T(1024)S(1)} %fusion.94) | copy-start | bytes 12292
  34.1 44.3 %copy-start.53 = (f32[768]{0:T(1024)}, f32[768]{0:T(1024)S(1)}, u32[]{:S(2)}) copy-start(f32[768]{0:T(1024)S(1)} %fusion.96) | copy-start | bytes 9220
  68.5 155.8 %collective-permute-start.3 = (bf16[2128,384]{1,0:T(8,128)(2,1)}, bf16[2128,384]{1,0:T(8,128)(2,1)}, u32[]{:S(2)}, u32[]{:S(2)}) collective-permute-start(bf16[2128,384]{1,0:T(8,128)(2,1)} %collective-permute-done.2), channel_id=1, source_target_pairs={{0,1},{1,0},{2,3},{3,2},{4,5},{5,4},{6,7},{7,6},{8,9},{9,8},{10,11... | collective-permute-start | bytes 4902920 | tf_op jit(solution)/shard_map/ppermute | solution.py:56
  302.2 160.5 %copy-start.37 = (f32[1024,32]{0,1:T(8,128)S(1)}, f32[1024,32]{0,1:T(8,128)}, u32[]{:S(2)}) copy-start(f32[1024,32]{0,1:T(8,128)} %copy-done.36) | copy-start | bytes 393220
  302.2 160.5 %copy-start.39 = (f32[1024,32]{0,1:T(8,128)S(1)}, f32[1024,32]{0,1:T(8,128)}, u32[]{:S(2)}) copy-start(f32[1024,32]{0,1:T(8,128)} %get-tuple-element.382) | copy-start | bytes 393220
  483.6 33.6 %collective-permute-start.4 = (bf16[2,1152,384]{1,2,0:T(8,128)(2,1)}, bf16[2,1152,384]{1,2,0:T(8,128)(2,1)}, u32[]{:S(2)}, u32[]{:S(2)}) collective-permute-start(bf16[2,1152,384]{1,2,0:T(8,128)(2,1)} %pad_maximum_fusion), channel_id=1, source_target_pairs={{0,1},{1,0},{2,3},{3,2},{4,5},{5,4},{6,7},{7,6},{8,9},{9,8},{10,11... | collective-permute-start | bytes 5308424 | tf_op jit(solution)/shard_map/ppermute | solution.py:56
  510.5 59.4 %collective-permute-start.13 = (bf16[2,2176,384]{1,2,0:T(8,128)(2,1)}, bf16[2,2176,384]{1,2,0:T(8,128)(2,1)}, u32[]{:S(2)}, u32[]{:S(2)}) collective-permute-start(bf16[2,2176,384]{1,2,0:T(8,128)(2,1)} %concatenate.218), channel_id=1, source_target_pairs={{0,1},{1,0},{2,3},{3,2},{4,5},{5,4},{6,7},{7,6},{8,9},{9,8},{10,11... | collective-permute-start | bytes 10027016 | tf_op jit(solution)/shard_map/ppermute | solution.py:56
  521.8 21.4 %collective-permute-start.5 = (bf16[1,1152,384]{1,2,0:T(8,128)(2,1)}, bf16[1,1152,384]{1,2,0:T(8,128)(2,1)}, u32[]{:S(2)}, u32[]{:S(2)}) collective-permute-start(bf16[1,1152,384]{1,2,0:T(8,128)(2,1)} %constant_dynamic-slice_fusion.22), channel_id=1, source_target_pairs={{0,16},{16,0},{1,17},{17,1},{2,18},{18,2},{3,19},{19,3},{4,20},{20... | collective-permute-start | bytes 2654216 | tf_op jit(solution)/shard_map/ppermute | solution.py:60
  546.7 19.4 %collective-permute-start.6 = (bf16[576,384]{0,1:T(8,128)(2,1)}, bf16[576,384]{0,1:T(8,128)(2,1)}, u32[]{:S(2)}, u32[]{:S(2)}) collective-permute-start(bf16[576,384]{0,1:T(8,128)(2,1)} %dynamic-slice_bitcast_fusion), channel_id=1, source_target_pairs={{0,2},{1,3},{2,0},{3,1},{4,6},{5,7},{6,4},{7,5},{8,10},{9,11},{10,... | collective-permute-start | bytes 1327112 | tf_op jit(solution)/shard_map/ppermute | solution.py:56
  568.6 9.3 %collective-permute-start.7 = (bf16[288,384]{0,1:T(8,128)(2,1)}, bf16[288,384]{0,1:T(8,128)(2,1)S(1)}, u32[]{:S(2)}, u32[]{:S(2)}) collective-permute-start(bf16[288,384]{0,1:T(8,128)(2,1)} %constant_dynamic-slice_fusion.21), channel_id=1, source_target_pairs={{0,4},{1,5},{2,6},{3,7},{4,0},{5,1},{6,2},{7,3},{8,12},{9,13},{10,... | collective-permute-start | bytes 663560 | tf_op jit(solution)/shard_map/ppermute | solution.py:56
  576.6 36.8 %collective-permute-start.14 = (bf16[1,2176,384]{1,2,0:T(8,128)(2,1)}, bf16[1,2176,384]{1,2,0:T(8,128)(2,1)}, u32[]{:S(2)}, u32[]{:S(2)}) collective-permute-start(bf16[1,2176,384]{1,2,0:T(8,128)(2,1)} %constant_dynamic-slice_fusion.13), channel_id=1, source_target_pairs={{0,16},{16,0},{1,17},{17,1},{2,18},{18,2},{3,19},{19,3},{4,20},{20... | collective-permute-start | bytes 5013512 | tf_op jit(solution)/shard_map/ppermute | solution.py:60
  579.1 34.3 %copy-start.11 = (bf16[2,2176,384]{1,2,0:T(8,128)(2,1)S(1)}, bf16[2,2176,384]{1,2,0:T(8,128)(2,1)}, u32[]{:S(2)}) copy-start(bf16[2,2176,384]{1,2,0:T(8,128)(2,1)} %copy-done.10) | copy-start | bytes 10027012
  579.1 12.2 %collective-permute-start.8 = (bf16[144,384]{0,1:T(8,128)(2,1)S(1)}, bf16[144,384]{0,1:T(8,128)(2,1)S(1)}, u32[]{:S(2)}, u32[]{:S(2)}) collective-permute-start(bf16[144,384]{0,1:T(8,128)(2,1)S(1)} %constant_dynamic-slice_fusion.20), channel_id=1, source_target_pairs={{0,8},{1,9},{2,10},{3,11},{4,12},{5,13},{6,14},{7,15},{8,0},{9,1},... | collective-permute-start | bytes 331784 | tf_op jit(solution)/shard_map/ppermute | solution.py:56
  591.5 35.9 %collective-permute-start.9 = (bf16[144,384]{0,1:T(8,128)(2,1)S(1)}, bf16[144,384]{0,1:T(8,128)(2,1)S(1)}, u32[]{:S(2)}, u32[]{:S(2)}) collective-permute-start(bf16[144,384]{0,1:T(8,128)(2,1)S(1)} %add_convert_fusion.12), channel_id=1, source_target_pairs={{0,8},{1,9},{2,10},{3,11},{4,12},{5,13},{6,14},{7,15},{8,0},{9,1},... | collective-permute-start | bytes 331784 | tf_op jit(solution)/shard_map/ppermute | solution.py:56
  620.0 18.1 %collective-permute-start.15 = (bf16[1088,384]{1,0:T(8,128)(2,1)}, bf16[1088,384]{1,0:T(8,128)(2,1)}, u32[]{:S(2)}, u32[]{:S(2)}) collective-permute-start(bf16[1088,384]{1,0:T(8,128)(2,1)} %bitcast.243), channel_id=1, source_target_pairs={{0,2},{1,3},{2,0},{3,1},{4,6},{5,7},{6,4},{7,5},{8,10},{9,11},{10,... | collective-permute-start | bytes 2506760 | tf_op jit(solution)/shard_map/ppermute | solution.py:56
  627.6 6.0 collective-permute-start.10
  634.8 18.8 %collective-permute-start.11 = (bf16[576,384]{0,1:T(8,128)(2,1)}, bf16[576,384]{0,1:T(8,128)(2,1)}, u32[]{:S(2)}, u32[]{:S(2)}) collective-permute-start(bf16[576,384]{0,1:T(8,128)(2,1)} %maximum_select_fusion.14), channel_id=1, source_target_pairs={{0,2},{1,3},{2,0},{3,1},{4,6},{5,7},{6,4},{7,5},{8,10},{9,11},{10,... | collective-permute-start | bytes 1327112 | tf_op jit(solution)/shard_map/ppermute | solution.py:56
  642.8 8.1 %collective-permute-start.16 = (bf16[544,384]{0,1:T(8,128)(2,1)S(1)}, bf16[544,384]{0,1:T(8,128)(2,1)S(1)}, u32[]{:S(2)}, u32[]{:S(2)}) collective-permute-start(bf16[544,384]{0,1:T(8,128)(2,1)S(1)} %constant_dynamic-slice_fusion.11), channel_id=1, source_target_pairs={{0,4},{1,5},{2,6},{3,7},{4,0},{5,1},{6,2},{7,3},{8,12},{9,13},{10,... | collective-permute-start | bytes 1253384 | tf_op jit(solution)/shard_map/ppermute | solution.py:56
  644.4 33.4 %copy-start.2 = (f32[1024,768]{0,1:T(8,128)S(1)}, f32[1024,768]{0,1:T(8,128)}, u32[]{:S(2)}) copy-start(f32[1024,768]{0,1:T(8,128)} %copy-done.1) | copy-start | bytes 9437188
  644.4 33.4 %copy-start.59 = (pred[1024]{0:T(1024)(128)(4,1)S(1)}, pred[1024]{0:T(1024)(128)(4,1)}, u32[]{:S(2)}) copy-start(pred[1024]{0:T(1024)(128)(4,1)} %iota_compare_fusion.3) | copy-start | bytes 3076
  651.4 15.5 %collective-permute-start.17 = (bf16[272,384]{0,1:T(8,128)(2,1)S(1)}, bf16[272,384]{0,1:T(8,128)(2,1)S(1)}, u32[]{:S(2)}, u32[]{:S(2)}) collective-permute-start(bf16[272,384]{0,1:T(8,128)(2,1)S(1)} %constant_dynamic-slice_fusion.10), channel_id=1, source_target_pairs={{0,8},{1,9},{2,10},{3,11},{4,12},{5,13},{6,14},{7,15},{8,0},{9,1},... | collective-permute-start | bytes 626696 | tf_op jit(solution)/shard_map/ppermute | solution.py:56
  656.5 78.1 %collective-permute-start.12 = (bf16[1152,384]{0,1:T(8,128)(2,1)}, bf16[1152,384]{0,1:T(8,128)(2,1)}, u32[]{:S(2)}, u32[]{:S(2)}) collective-permute-start(bf16[1152,384]{0,1:T(8,128)(2,1)} %maximum_select_fusion.8), channel_id=1, source_target_pairs={{0,1},{1,0},{2,3},{3,2},{4,5},{5,4},{6,7},{7,6},{8,9},{9,8},{10,11... | collective-permute-start | bytes 2654216 | tf_op jit(solution)/shard_map/ppermute | solution.py:56
  667.1 9.4 %collective-permute-start.18 = (bf16[272,384]{0,1:T(8,128)(2,1)S(1)}, bf16[272,384]{0,1:T(8,128)(2,1)S(1)}, u32[]{:S(2)}, u32[]{:S(2)}) collective-permute-start(bf16[272,384]{0,1:T(8,128)(2,1)S(1)} %add_convert_fusion.10), channel_id=1, source_target_pairs={{0,8},{1,9},{2,10},{3,11},{4,12},{5,13},{6,14},{7,15},{8,0},{9,1},... | collective-permute-start | bytes 626696 | tf_op jit(solution)/shard_map/ppermute | solution.py:56
  677.7 58.7 %collective-permute-start.19 = (bf16[544,384]{0,1:T(8,128)(2,1)}, bf16[544,384]{0,1:T(8,128)(2,1)}, u32[]{:S(2)}, u32[]{:S(2)}) collective-permute-start(bf16[544,384]{0,1:T(8,128)(2,1)} %maximum_select_fusion.15), channel_id=1, source_target_pairs={{0,4},{1,5},{2,6},{3,7},{4,0},{5,1},{6,2},{7,3},{8,12},{9,13},{10,... | collective-permute-start | bytes 1253384 | tf_op jit(solution)/shard_map/ppermute | solution.py:56
  739.8 19.8 %collective-permute-start.20 = (bf16[1088,384]{1,0:T(8,128)(2,1)S(1)}, bf16[1088,384]{1,0:T(8,128)(2,1)}, u32[]{:S(2)}, u32[]{:S(2)}) collective-permute-start(bf16[1088,384]{1,0:T(8,128)(2,1)S(1)} %copy.225), channel_id=1, source_target_pairs={{0,2},{1,3},{2,0},{3,1},{4,6},{5,7},{6,4},{7,5},{8,10},{9,11},{10,... | collective-permute-start | bytes 2506760 | tf_op jit(solution)/shard_map/ppermute | solution.py:56
  763.6 13.7 %collective-permute-start.21 = (bf16[2176,384]{0,1:T(8,128)(2,1)}, bf16[2176,384]{0,1:T(8,128)(2,1)}, u32[]{:S(2)}, u32[]{:S(2)}) collective-permute-start(bf16[2176,384]{0,1:T(8,128)(2,1)} %maximum_select_fusion.4), channel_id=1, source_target_pairs={{0,1},{1,0},{2,3},{3,2},{4,5},{5,4},{6,7},{7,6},{8,9},{9,8},{10,11... | collective-permute-start | bytes 5013512 | tf_op jit(solution)/shard_map/ppermute | solution.py:56
  (65 other events, 232.5 us)
where the time goes:
time: 815 us; the launch traced here: 799 us
  matrix products  270 us (33%)
  local copies, waits for them, and re-layouts  241 us (30%)
  waiting for transfers between devices  104 us (13%)
  other arithmetic  102 us (13%)
  blocking collectives  47.6 us (6%)
  starting transfers between devices  31.5 us (4%)
    unnamed x179, local copies, waits for them, and re-layouts  93.2 us
    ppermute x4, waiting for transfers between devices, swap_group(): return lax.ppermute(field, 'group', [(0, 1), (1, 0)])  69 us
    dot_general x24, matrix products, masked_scores(): jnp.einsum('qd,kd->qk', head_query, head_keys, preferred_element_type=jnp...  53.4 us
    psum x1, blocking collectives, on_device(): gains = lax.psum(gains, ('group', 'replica'))  47.6 us
    dot_general x12, matrix products, forward_head(): jnp.einsum('qk,kd->qd', weights.astype(jnp.bfloat16), head_values, prefer...  41.5 us
    dot_general x4, matrix products, outer(): lax.dot_general(left, right, (((1,), (1,)), ((), ())), preferred_element_...  38.9 us
    ppermute x18, waiting for transfers between devices, swap_replica(): return lax.ppermute(field, 'replica', [(i, i ^ bit) for i in range(count)])  34.6 us
    reshape x16, local copies, waits for them, and re-layouts, unit_of(): parts.append(part[:, i * wide:(i + 1) * wide].reshape(2, rows, wide))  33.3 us
  transfers between devices with their start and end apart: 22, of which 8 were waited for; matrix products, arithmetic and copies ran while one was open for 36% of the time, Pallas kernels for 0%

commit v1 on v0

--- a/solution.py
+++ b/solution.py
@@ -280,7 +280,7 @@
     grad_down, grad_in, grad_out = spread(early_sum, early)
     (grad_qkv,) = spread(late_sum, late)
     gains = jnp.stack([grad_gain_one, grad_gain_two])
-    gains = lax.psum(gains, ("group", "replica"))
+    gains = jnp.sum(lax.all_gather(gains, ("group", "replica")), axis=0)
     gains = lax.dynamic_slice_in_dim(gains, group * n_own, n_own, 1)
     return (output, grad_tokens, grad_qkv, grad_out, gains[0], grad_in, grad_down, gains[1])
 

time: 815 us -> 754 us (0.925)
  local copies, waits for them, and re-layouts: 241 us -> 206 us
  starting transfers between devices: 31.5 us -> 23.3 us
    psum x1 -> x0, blocking collectives: 47.6 us -> none  [on_device(): gains = lax.psum(gains, ('group', 'replica'))]
    all_gather x0 -> x1, blocking collectives: none -> 46.4 us  [on_device(): gains = jnp.sum(lax.all_gather(gains, ('group', 'replica')), axis=0)]
    ppermute x4, waiting for transfers between devices: 69 us -> 46.7 us  [swap_group(): return lax.ppermute(field, 'group', [(0, 1), (1, 0)])]
    ppermute x18, waiting for transfers between devices: 34.6 us -> 53.2 us  [swap_replica(): return lax.ppermute(field, 'replica', [(i, i ^ bit) for i in range(count)])]
    dynamic_update_slice x12, local copies, waits for them, and re-layouts: 16.8 us -> 1.32 us  [on_device(): heads, log_totals = lax.map(forward_head, (query, key_rows, values))]
    dynamic_slice x12, local copies, waits for them, and re-layouts: 9.25 us -> 0.16 us  [on_device(): lax.map(backward_head, (query, key_rows, values, d_heads, log_totals))]
    ppermute x18, starting transfers between devices: 26.8 us -> 18.5 us  [swap_replica(): return lax.ppermute(field, 'replica', [(i, i ^ bit) for i in range(count)])]
    unnamed x179 -> x169, local copies, waits for them, and re-layouts: 93.2 us -> 91.6 us
  transfers between devices with their start and end apart: 22 -> 22, of which waited for: 8 -> 9; matrix products, arithmetic and copies ran while one was open for 36% -> 35% of each run, Pallas kernels for 0% -> 0%
where the time goes in v1:
time: 754 us; the launch traced here: 741 us
  matrix products  266 us (35%)
  local copies, waits for them, and re-layouts  206 us (27%)
  waiting for transfers between devices  99.9 us (13%)
  other arithmetic  94.6 us (13%)
  blocking collectives  46.4 us (6%)
  starting transfers between devices  23.3 us (3%)
    unnamed x169, local copies, waits for them, and re-layouts  91.6 us
    dot_general x24, matrix products, masked_scores(): jnp.einsum('qd,kd->qk', head_query, head_keys, preferred_element_type=jnp...  53.4 us
    ppermute x18, waiting for transfers between devices, swap_replica(): return lax.ppermute(field, 'replica', [(i, i ^ bit) for i in range(count)])  53.2 us
    ppermute x4, waiting for transfers between devices, swap_group(): return lax.ppermute(field, 'group', [(0, 1), (1, 0)])  46.7 us
    all_gather x1, blocking collectives, on_device(): gains = jnp.sum(lax.all_gather(gains, ('group', 'replica')), axis=0)  46.4 us
    dot_general x12, matrix products, forward_head(): jnp.einsum('qk,kd->qd', weights.astype(jnp.bfloat16), head_values, prefer...  41.6 us
    dot_general x4, matrix products, outer(): lax.dot_general(left, right, (((1,), (1,)), ((), ())), preferred_element_...  34.6 us
    reshape x16, local copies, waits for them, and re-layouts, unit_of(): parts.append(part[:, i * wide:(i + 1) * wide].reshape(2, rows, wide))  29.8 us
  transfers between devices with their start and end apart: 22, of which 9 were waited for; matrix products, arithmetic and copies ran while one was open for 35% of the time, Pallas kernels for 0%

profile of v1, /device:TPU:1, one launch (start us, length us, event | category | flops | bytes accessed | tf_op | source)
XLA Modules:
  0.0 740.5 jit_solution(5660760648274779998)
XLA Ops:
  11.8 4.3 copy.179
  18.3 3.9 copy.195
  34.6 26.8 %collective-permute-done.2 = bf16[2128,384]{1,0:T(8,128)(2,1)} collective-permute-done((bf16[2128,384]{1,0:T(8,128)(2,1)}, bf16[2128,384]{1,0:T(8,128)(2,1)}, u32[]{:S(2)}, u32[]{:S(2)}) %collective-permute-start.2) | collective-permute-done | bytes 1634336 | tf_op jit(solution)/shard_map/ppermute | solution.py:60
  80.1 4.1 convolution_bitcast_fusion
  96.6 4.2 copy.184
  100.8 107.4 %while.30 = (s32[]{:T(128)}, bf16[12,1024,64]{1,2,0:T(8,128)(2,1)S(1)}, f32[12,1024]{1,0:T(8,128)S(1)}, bf16[12,1024,64]{2,1,0:T(8,128)(2,1)}, bf16[12,1024,64]{...) while((s32[]{:T(128)}, bf16[12,1024,64]{1,2,0:T(8,128)(2,1)S(1)}, ...), condition=%wide.region_5.6_spmd.clone.clone, body=%wide.region_2.5_spmd.clone.sunk.clone | while | flops 281018368 | bytes 30455920 | solution.py:178
  151.0 3.5 fusion.162
  160.0 3.5 fusion.162
  168.9 3.5 fusion.162
  177.9 3.5 fusion.162
  230.8 4.3 fusion.87
  235.1 15.0 %fusion.78 = (f32[1024,1152]{1,0:T(8,128)}, f32[1024,1152]{1,0:T(8,128)S(1)}, f32[1024,1152]{1,0:T(8,128)S(1)}) fusion(f32[1024,2304]{1,0:T(8,128)S(1)} %fusion.87, bf16[576,768]{0,1:T(8,128)(2,1)S(1)} %maximum_select_fusion.6, bf16[576,768]{0,1:T(8,128)(2,1)S(1)} %copy-done.41, pred[]{:T(512)S(6)} %eq.18, bf16[1,1024,768]{1,2,0:T(8,128)(2,1)S(1)} %copy-done.8, ...), kind=kOutput, calls=%fused_computation.147 | convolution fusion | flops 1897365504 | bytes 22217728 | tf_op jit(solution)/shard_map/dot_general | solution.py:49
  250.1 4.6 multiply_add_fusion
  254.7 12.1 %multiply_reduce_fusion.1 = (f32[768]{0:T(1024)S(1)}, f32[1024]{0:T(1024)S(1)}, f32[1024,768]{0,1:T(8,128)}) fusion(f32[1024,768]{0,1:T(8,128)S(1)} %copy-done.12, f32[1024]{0:T(1024)S(1)} %fusion.95, f32[1024]{0:T(1024)S(1)} %broadcast_multiply_fusion, f32[768]{0:T(1024)S(1)} %fusion.97, bf16[384,2304]{0,1:T(8,128)(2,1)} %copy-done.29, ...), kind=kOutput, calls=%fused_computation.109 | convolution fusion | flops 3650025728 | bytes 19286016 | tf_op jit(solution)/shard_map/dot_general | solution.py:49
  266.8 9.6 %convolution_convert_fusion = bf16[768,2304]{1,0:T(8,128)(2,1)} fusion(f32[1024,1152]{1,0:T(8,128)} %get-tuple-element.318, f32[1024,1152]{1,0:T(8,128)} %get-tuple-element.312, f32[1024,768]{0,1:T(8,128)S(1)} %copy-done.12, f32[768]{0:T(1024)S(1)} %fusion.97, f32[1024]{0:T(1024)S(1)} %fusion.95, f32[1024]{0:T(1024)S(1)} %broadcast_multiply_fusion), kind=kOutput, calls=%fused_computation.62 | convolution fusion | flops 3633512448 | bytes 16133120 | tf_op jit(solution)/shard_map/dot_general | solution.py:43
  285.7 151.6 %while.31 = (s32[]{:T(128)}, f32[12,1024,64]{1,2,0:T(8,128)}, f32[12,1024,64]{1,2,0:T(8,128)}, bf16[12,1024,64]{1,2,0:T(8,128)(2,1)S(1)}, bf16[12,1024,64]{2,1,0...) while((s32[]{:T(128)}, f32[12,1024,64]{1,2,0:T(8,128)}, ...), condition=%wide.region_12.13_spmd.clone.clone, body=%wide.region_10.12_spmd.clone.sunk.clone | while | flops 681705472 | bytes 34106476 | solution.py:223
  437.4 3.8 multiply_add_fusion.4
  443.1 4.8 convolution_convert_fusion.1
  464.0 3.7 convolution_convert_fusion.2
  471.4 6.9 concatenate.218
  501.5 7.1 concatenate.217
  518.0 5.8 collective-permute-done.6
  525.8 6.0 fusion.66
  535.1 18.1 %collective-permute-done.14 = bf16[1,2176,384]{1,2,0:T(8,128)(2,1)S(1)} collective-permute-done((bf16[1,2176,384]{1,2,0:T(8,128)(2,1)S(1)}, bf16[1,2176,384]{1,2,0:T(8,128)(2,1)S(1)}, u32[]{:S(2)}, u32[]{:S(2)}) %collective-permute-start.14) | collective-permute-done | bytes 1671200 | tf_op jit(solution)/shard_map/ppermute | solution.py:60
  558.5 7.4 fusion.79
  569.5 8.5 %collective-permute-done.9 = bf16[144,384]{0,1:T(8,128)(2,1)S(1)} collective-permute-done((bf16[144,384]{0,1:T(8,128)(2,1)S(1)}, bf16[144,384]{0,1:T(8,128)(2,1)S(1)}, u32[]{:S(2)}, u32[]{:S(2)}) %collective-permute-start.9) | collective-permute-done | bytes 110624 | tf_op jit(solution)/shard_map/ppermute | solution.py:56
  588.7 7.9 %collective-permute-done.16 = bf16[544,384]{0,1:T(8,128)(2,1)S(1)} collective-permute-done((bf16[544,384]{0,1:T(8,128)(2,1)S(1)}, bf16[544,384]{0,1:T(8,128)(2,1)S(1)}, u32[]{:S(2)}, u32[]{:S(2)}) %collective-permute-start.16) | collective-permute-done | bytes 417824 | tf_op jit(solution)/shard_map/ppermute | solution.py:56
  602.7 10.1 %collective-permute-done.17 = bf16[272,384]{0,1:T(8,128)(2,1)S(1)} collective-permute-done((bf16[272,384]{0,1:T(8,128)(2,1)S(1)}, bf16[272,384]{0,1:T(8,128)(2,1)S(1)}, u32[]{:S(2)}, u32[]{:S(2)}) %collective-permute-start.17) | collective-permute-done | bytes 208928 | tf_op jit(solution)/shard_map/ppermute | solution.py:56
  616.3 3.7 copy.229
  621.6 7.7 %collective-permute-done.18 = bf16[272,384]{0,1:T(8,128)(2,1)} collective-permute-done((bf16[272,384]{0,1:T(8,128)(2,1)S(1)}, bf16[272,384]{0,1:T(8,128)(2,1)}, u32[]{:S(2)}, u32[]{:S(2)}) %collective-permute-start.18) | collective-permute-done | bytes 208928 | tf_op jit(solution)/shard_map/ppermute | solution.py:56
  630.7 46.4 %all-gather.1 = f32[32,2,768]{2,1,0:T(2,128)S(1)} all-gather(f32[1,2,768]{2,1,0:T(2,128)S(1)} %maximum_bitcast_fusion), channel_id=2, replica_groups=mesh['group'=2,'replica'=16] {'group','replica'}, dimensions={0}, use_global_device_ids=true | all-gather | bytes 202752 | tf_op jit(solution)/shard_map/all_gather | solution.py:283
  688.8 13.2 %collective-permute-done.20 = bf16[1088,384]{1,0:T(8,128)(2,1)} collective-permute-done((bf16[1088,384]{1,0:T(8,128)(2,1)S(1)}, bf16[1088,384]{1,0:T(8,128)(2,1)}, u32[]{:S(2)}, u32[]{:S(2)}) %collective-permute-start.20) | collective-permute-done | bytes 835616 | tf_op jit(solution)/shard_map/ppermute | solution.py:56
  (510 shorter events, 472.5 us)
Async XLA Ops:
  3.9 26.4 %collective-permute-start = (bf16[400,1152]{1,0:T(8,128)(2,1)}, bf16[400,1152]{1,0:T(8,128)(2,1)}, u32[]{:S(2)}, u32[]{:S(2)}) collective-permute-start(bf16[400,1152]{1,0:T(8,128)(2,1)} %fusion.83), channel_id=1, source_target_pairs={{0,16},{16,0},{1,17},{17,1},{2,18},{18,2},{3,19},{19,3},{4,20},{20... | collective-permute-start | bytes 2764808 | tf_op jit(solution)/shard_map/ppermute | solution.py:60
  10.3 51.1 %collective-permute-start.2 = (bf16[2128,384]{1,0:T(8,128)(2,1)}, bf16[2128,384]{1,0:T(8,128)(2,1)}, u32[]{:S(2)}, u32[]{:S(2)}) collective-permute-start(bf16[2128,384]{1,0:T(8,128)(2,1)} %constant_dynamic-update-slice_fusion), channel_id=1, source_target_pairs={{0,16},{16,0},{1,17},{17,1},{2,18},{18,2},{3,19},{19,3},{4,20},{20... | collective-permute-start | bytes 4902920 | tf_op jit(solution)/shard_map/ppermute | solution.py:60
  25.2 188.4 %copy-start.1 = (bf16[1,1024,768]{1,2,0:T(8,128)(2,1)}, bf16[1,1024,768]{1,2,0:T(8,128)(2,1)S(1)}, u32[]{:S(2)}) copy-start(bf16[1,1024,768]{1,2,0:T(8,128)(2,1)S(1)} %copy.176) | copy-start | bytes 4718596
  28.6 49.7 %copy-start.46 = (f32[1024]{0:T(1024)}, f32[1024]{0:T(1024)S(1)}, u32[]{:S(2)}) copy-start(f32[1024]{0:T(1024)S(1)} %broadcast_multiply_fusion.1) | copy-start | bytes 12292
  30.3 56.4 %copy-start.32 = (f32[1024,32]{0,1:T(8,128)}, f32[1024,32]{0,1:T(8,128)S(1)}, u32[]{:S(2)}) copy-start(f32[1024,32]{0,1:T(8,128)S(1)} %get-tuple-element.381) | copy-start | bytes 393220
  30.3 40.1 %collective-permute-start.1 = (bf16[400,1152]{1,0:T(8,128)(2,1)}, bf16[400,1152]{1,0:T(8,128)(2,1)}, u32[]{:S(2)}, u32[]{:S(2)}) collective-permute-start(bf16[400,1152]{1,0:T(8,128)(2,1)} %collective-permute-done), channel_id=1, source_target_pairs={{0,1},{1,0},{2,3},{3,2},{4,5},{5,4},{6,7},{7,6},{8,9},{9,8},{10,11... | collective-permute-start | bytes 2764808 | tf_op jit(solution)/shard_map/ppermute | solution.py:56
  31.3 47.1 %copy-start.48 = (f32[1024]{0:T(1024)}, f32[1024]{0:T(1024)S(1)}, u32[]{:S(2)}) copy-start(f32[1024]{0:T(1024)S(1)} %fusion.94) | copy-start | bytes 12292
  34.6 43.8 %copy-start.50 = (f32[768]{0:T(1024)}, f32[768]{0:T(1024)S(1)}, u32[]{:S(2)}) copy-start(f32[768]{0:T(1024)S(1)} %fusion.96) | copy-start | bytes 9220
  68.5 139.7 %collective-permute-start.3 = (bf16[2128,384]{1,0:T(8,128)(2,1)}, bf16[2128,384]{1,0:T(8,128)(2,1)}, u32[]{:S(2)}, u32[]{:S(2)}) collective-permute-start(bf16[2128,384]{1,0:T(8,128)(2,1)} %collective-permute-done.2), channel_id=1, source_target_pairs={{0,1},{1,0},{2,3},{3,2},{4,5},{5,4},{6,7},{7,6},{8,9},{9,8},{10,11... | collective-permute-start | bytes 4902920 | tf_op jit(solution)/shard_map/ppermute | solution.py:56
  285.7 151.6 %copy-start.33 = (f32[1024,32]{0,1:T(8,128)S(1)}, f32[1024,32]{0,1:T(8,128)}, u32[]{:S(2)}) copy-start(f32[1024,32]{0,1:T(8,128)} %copy-done.32) | copy-start | bytes 393220
  285.7 151.6 %copy-start.35 = (f32[1024,32]{0,1:T(8,128)S(1)}, f32[1024,32]{0,1:T(8,128)}, u32[]{:S(2)}) copy-start(f32[1024,32]{0,1:T(8,128)} %get-tuple-element.382) | copy-start | bytes 393220
  454.0 30.8 %collective-permute-start.4 = (bf16[2,1152,384]{1,2,0:T(8,128)(2,1)}, bf16[2,1152,384]{1,2,0:T(8,128)(2,1)}, u32[]{:S(2)}, u32[]{:S(2)}) collective-permute-start(bf16[2,1152,384]{1,2,0:T(8,128)(2,1)} %pad_maximum_fusion), channel_id=1, source_target_pairs={{0,1},{1,0},{2,3},{3,2},{4,5},{5,4},{6,7},{7,6},{8,9},{9,8},{10,11... | collective-permute-start | bytes 5308424 | tf_op jit(solution)/shard_map/ppermute | solution.py:56
  478.4 35.5 %collective-permute-start.13 = (bf16[2,2176,384]{1,2,0:T(8,128)(2,1)}, bf16[2,2176,384]{1,2,0:T(8,128)(2,1)}, u32[]{:S(2)}, u32[]{:S(2)}) collective-permute-start(bf16[2,2176,384]{1,2,0:T(8,128)(2,1)} %concatenate.218), channel_id=1, source_target_pairs={{0,1},{1,0},{2,3},{3,2},{4,5},{5,4},{6,7},{7,6},{8,9},{9,8},{10,11... | collective-permute-start | bytes 10027016 | tf_op jit(solution)/shard_map/ppermute | solution.py:56
  489.3 21.0 %collective-permute-start.5 = (bf16[1,1152,384]{1,2,0:T(8,128)(2,1)}, bf16[1,1152,384]{1,2,0:T(8,128)(2,1)}, u32[]{:S(2)}, u32[]{:S(2)}) collective-permute-start(bf16[1,1152,384]{1,2,0:T(8,128)(2,1)} %constant_dynamic-slice_fusion.22), channel_id=1, source_target_pairs={{0,16},{16,0},{1,17},{17,1},{2,18},{18,2},{3,19},{19,3},{4,20},{20... | collective-permute-start | bytes 2654216 | tf_op jit(solution)/shard_map/ppermute | solution.py:60
  512.0 13.8 %slice-start = ((s8[4718592]{0:T(1024)(128)(4,1)}), s8[4194304]{0:T(1024)(128)(4,1)S(1)}, s32[]{:S(2)}) async-start(s8[4718592]{0:T(1024)(128)(4,1)} %bitcast.226), calls=%async_computation | async-start | bytes 8388608
  512.3 13.6 %slice-start.1 = ((s8[4718592]{0:T(1024)(128)(4,1)}), s8[524288]{0:T(1024)(128)(4,1)S(1)}, s32[]{:S(2)}) async-start(s8[4718592]{0:T(1024)(128)(4,1)} %bitcast.226), calls=%async_computation.1 | async-start | bytes 1048576
  512.3 11.6 %collective-permute-start.6 = (bf16[576,384]{0,1:T(8,128)(2,1)S(1)}, bf16[576,384]{0,1:T(8,128)(2,1)S(1)}, u32[]{:S(2)}, u32[]{:S(2)}) collective-permute-start(bf16[576,384]{0,1:T(8,128)(2,1)S(1)} %dynamic-slice_bitcast_fusion), channel_id=1, source_target_pairs={{0,2},{1,3},{2,0},{3,1},{4,6},{5,7},{6,4},{7,5},{8,10},{9,11},{10,... | collective-permute-start | bytes 1327112 | tf_op jit(solution)/shard_map/ppermute | solution.py:56
  516.7 36.5 %collective-permute-start.14 = (bf16[1,2176,384]{1,2,0:T(8,128)(2,1)S(1)}, bf16[1,2176,384]{1,2,0:T(8,128)(2,1)S(1)}, u32[]{:S(2)}, u32[]{:S(2)}) collective-permute-start(bf16[1,2176,384]{1,2,0:T(8,128)(2,1)S(1)} %constant_dynamic-slice_fusion.13), channel_id=1, source_target_pairs={{0,16},{16,0},{1,17},{17,1},{2,18},{18,2},{3,19},{19,3},{4,20},{20... | collective-permute-start | bytes 5013512 | tf_op jit(solution)/shard_map/ppermute | solution.py:60
  524.3 7.6 %collective-permute-start.7 = (bf16[288,384]{0,1:T(8,128)(2,1)S(1)}, bf16[288,384]{0,1:T(8,128)(2,1)S(1)}, u32[]{:S(2)}, u32[]{:S(2)}) collective-permute-start(bf16[288,384]{0,1:T(8,128)(2,1)S(1)} %constant_dynamic-slice_fusion.21), channel_id=1, source_target_pairs={{0,4},{1,5},{2,6},{3,7},{4,0},{5,1},{6,2},{7,3},{8,12},{9,13},{10,... | collective-permute-start | bytes 663560 | tf_op jit(solution)/shard_map/ppermute | solution.py:56
  532.8 33.1 %collective-permute-start.8 = (bf16[144,384]{0,1:T(8,128)(2,1)}, bf16[144,384]{0,1:T(8,128)(2,1)}, u32[]{:S(2)}, u32[]{:S(2)}) collective-permute-start(bf16[144,384]{0,1:T(8,128)(2,1)} %constant_dynamic-slice_fusion.20), channel_id=1, source_target_pairs={{0,8},{1,9},{2,10},{3,11},{4,12},{5,13},{6,14},{7,15},{8,0},{9,1},... | collective-permute-start | bytes 331784 | tf_op jit(solution)/shard_map/ppermute | solution.py:56
  558.3 20.3 %collective-permute-start.15 = (bf16[1088,384]{1,0:T(8,128)(2,1)}, bf16[1088,384]{1,0:T(8,128)(2,1)}, u32[]{:S(2)}, u32[]{:S(2)}) collective-permute-start(bf16[1088,384]{1,0:T(8,128)(2,1)} %bitcast.247), channel_id=1, source_target_pairs={{0,2},{1,3},{2,0},{3,1},{4,6},{5,7},{6,4},{7,5},{8,10},{9,11},{10,... | collective-permute-start | bytes 2506760 | tf_op jit(solution)/shard_map/ppermute | solution.py:56
  567.0 11.0 %collective-permute-start.9 = (bf16[144,384]{0,1:T(8,128)(2,1)S(1)}, bf16[144,384]{0,1:T(8,128)(2,1)S(1)}, u32[]{:S(2)}, u32[]{:S(2)}) collective-permute-start(bf16[144,384]{0,1:T(8,128)(2,1)S(1)} %add_convert_fusion.12), channel_id=1, source_target_pairs={{0,8},{1,9},{2,10},{3,11},{4,12},{5,13},{6,14},{7,15},{8,0},{9,1},... | collective-permute-start | bytes 331784 | tf_op jit(solution)/shard_map/ppermute | solution.py:56
  578.3 7.7 %collective-permute-start.10 = (bf16[288,384]{0,1:T(8,128)(2,1)S(1)}, bf16[288,384]{0,1:T(8,128)(2,1)}, u32[]{:S(2)}, u32[]{:S(2)}) collective-permute-start(bf16[288,384]{0,1:T(8,128)(2,1)S(1)} %maximum_select_fusion.16), channel_id=1, source_target_pairs={{0,4},{1,5},{2,6},{3,7},{4,0},{5,1},{6,2},{7,3},{8,12},{9,13},{10,... | collective-permute-start | bytes 663560 | tf_op jit(solution)/shard_map/ppermute | solution.py:56
  583.3 13.3 %collective-permute-start.16 = (bf16[544,384]{0,1:T(8,128)(2,1)S(1)}, bf16[544,384]{0,1:T(8,128)(2,1)S(1)}, u32[]{:S(2)}, u32[]{:S(2)}) collective-permute-start(bf16[544,384]{0,1:T(8,128)(2,1)S(1)} %constant_dynamic-slice_fusion.11), channel_id=1, source_target_pairs={{0,4},{1,5},{2,6},{3,7},{4,0},{5,1},{6,2},{7,3},{8,12},{9,13},{10,... | collective-permute-start | bytes 1253384 | tf_op jit(solution)/shard_map/ppermute | solution.py:56
  585.9 27.1 %copy-start.4 = (f32[1024,768]{0,1:T(8,128)S(1)}, f32[1024,768]{0,1:T(8,128)}, u32[]{:S(2)}) copy-start(f32[1024,768]{0,1:T(8,128)} %copy-done.3) | copy-start | bytes 9437188
  587.5 10.6 %collective-permute-start.11 = (bf16[576,384]{0,1:T(8,128)(2,1)S(1)}, bf16[576,384]{0,1:T(8,128)(2,1)S(1)}, u32[]{:S(2)}, u32[]{:S(2)}) collective-permute-start(bf16[576,384]{0,1:T(8,128)(2,1)S(1)} %maximum_select_fusion.14), channel_id=1, source_target_pairs={{0,2},{1,3},{2,0},{3,1},{4,6},{5,7},{6,4},{7,5},{8,10},{9,11},{10,... | collective-permute-start | bytes 1327112 | tf_op jit(solution)/shard_map/ppermute | solution.py:56
  597.1 15.7 %collective-permute-start.17 = (bf16[272,384]{0,1:T(8,128)(2,1)S(1)}, bf16[272,384]{0,1:T(8,128)(2,1)S(1)}, u32[]{:S(2)}, u32[]{:S(2)}) collective-permute-start(bf16[272,384]{0,1:T(8,128)(2,1)S(1)} %constant_dynamic-slice_fusion.10), channel_id=1, source_target_pairs={{0,8},{1,9},{2,10},{3,11},{4,12},{5,13},{6,14},{7,15},{8,0},{9,1},... | collective-permute-start | bytes 626696 | tf_op jit(solution)/shard_map/ppermute | solution.py:56
  599.6 78.3 %collective-permute-start.12 = (bf16[1152,384]{0,1:T(8,128)(2,1)}, bf16[1152,384]{0,1:T(8,128)(2,1)}, u32[]{:S(2)}, u32[]{:S(2)}) collective-permute-start(bf16[1152,384]{0,1:T(8,128)(2,1)} %maximum_select_fusion.8), channel_id=1, source_target_pairs={{0,1},{1,0},{2,3},{3,2},{4,5},{5,4},{6,7},{7,6},{8,9},{9,8},{10,11... | collective-permute-start | bytes 2654216 | tf_op jit(solution)/shard_map/ppermute | solution.py:56
  613.0 16.3 %collective-permute-start.18 = (bf16[272,384]{0,1:T(8,128)(2,1)S(1)}, bf16[272,384]{0,1:T(8,128)(2,1)}, u32[]{:S(2)}, u32[]{:S(2)}) collective-permute-start(bf16[272,384]{0,1:T(8,128)(2,1)S(1)} %add_convert_fusion.10), channel_id=1, source_target_pairs={{0,8},{1,9},{2,10},{3,11},{4,12},{5,13},{6,14},{7,15},{8,0},{9,1},... | collective-permute-start | bytes 626696 | tf_op jit(solution)/shard_map/ppermute | solution.py:56
  630.6 49.0 %collective-permute-start.19 = (bf16[544,384]{0,1:T(8,128)(2,1)S(1)}, bf16[544,384]{0,1:T(8,128)(2,1)S(1)}, u32[]{:S(2)}, u32[]{:S(2)}) collective-permute-start(bf16[544,384]{0,1:T(8,128)(2,1)S(1)} %maximum_select_fusion.15), channel_id=1, source_target_pairs={{0,4},{1,5},{2,6},{3,7},{4,0},{5,1},{6,2},{7,3},{8,12},{9,13},{10,... | collective-permute-start | bytes 1253384 | tf_op jit(solution)/shard_map/ppermute | solution.py:56
  681.8 20.2 %collective-permute-start.20 = (bf16[1088,384]{1,0:T(8,128)(2,1)S(1)}, bf16[1088,384]{1,0:T(8,128)(2,1)}, u32[]{:S(2)}, u32[]{:S(2)}) collective-permute-start(bf16[1088,384]{1,0:T(8,128)(2,1)S(1)} %copy.225), channel_id=1, source_target_pairs={{0,2},{1,3},{2,0},{3,1},{4,6},{5,7},{6,4},{7,5},{8,10},{9,11},{10,... | collective-permute-start | bytes 2506760 | tf_op jit(solution)/shard_map/ppermute | solution.py:56
  706.0 12.8 %collective-permute-start.21 = (bf16[2176,384]{0,1:T(8,128)(2,1)}, bf16[2176,384]{0,1:T(8,128)(2,1)}, u32[]{:S(2)}, u32[]{:S(2)}) collective-permute-start(bf16[2176,384]{0,1:T(8,128)(2,1)} %maximum_select_fusion.4), channel_id=1, source_target_pairs={{0,1},{1,0},{2,3},{3,2},{4,5},{5,4},{6,7},{7,6},{8,9},{9,8},{10,11... | collective-permute-start | bytes 5013512 | tf_op jit(solution)/shard_map/ppermute | solution.py:56
  (60 other events, 221.3 us)
